TPU v7x, 128 devices: a whole 4x4x4 slice. The times are simulated.
128 devices in a mesh: row: 16 (over z, x), vec: 8 (over y, core).
Axes of the slice: x: 4, y: 4, z: 4, core: 2. Of those that a mesh axis runs over, the one named last changes fastest.
Arguments:
- vectors: float32 [32768, 1024], P('row', 'vec'), may hold values from -8 to 8
- hamiltonian: float32 [256, 12, 128, 128], P('row'), may hold values from -0.15 to 0.15, as said below
- column_blocks: int32 [256, 12], P('row'), may hold values from 0 to 255, as said below
- live_counts: int32 [256], P('row'), may hold values from 3 to 12
- lower_bound: float32 [1], replicated, may hold values from -0.85 to -0.65
- upper_bound: float32 [1], replicated, may hold values from 1.05 to 1.3
Outputs:
- filtered: float32 [32768, 1024], P('row', 'vec')
Inputs may be any that keep to these rules, and one draw needn't show every extreme that they name: column_blocks[i, 0] = i, and every entry lies within 16 block rows of its row i, cyclically modulo 256; the distances 16 and -16 both occur. `hamiltonian`: H is symmetric: for every used slot of block row i that names column block j there is a used slot of block row j that names i and holds the transpose of its block, and slot 0 of every block row holds a symmetric block.
All inputs are finite; a program needn't handle non-finite values.
Results may differ from a plain program's by a relative error of at most 0.0003.
Values sent between devices are 32-bit elements; how exact they have to be, the bound alone decides.
No kernel may reach another device: no remote copies, remote signals or barrier semaphores. Data moves between devices by JAX's collectives and lax.ppermute only.
A program may use at most 128 MiB of HBM per device.

v0:
```python
import math
import jax
import jax.numpy as jnp
from jax import lax
from jax.sharding import PartitionSpec as P

NV = 1024
NS_ITERS = 3


def with_halo(cells, sides, width):
    for axis, dim in sides:
        count = lax.axis_size(axis)
        head = lax.slice_in_dim(cells, 0, width, axis=dim)
        tail = lax.slice_in_dim(cells, cells.shape[dim] - width, cells.shape[dim], axis=dim)
        cells = jnp.concatenate(
            [
                lax.ppermute(tail, axis, [(i, (i + 1) % count) for i in range(count)]),
                cells,
                lax.ppermute(head, axis, [((i + 1) % count, i) for i in range(count)]),
            ],
            axis=dim,
        )
    return cells


def on_device(vectors, hamiltonian, column_blocks, live_counts, lower_bound, upper_bound):
    rows_dev, panel_cols = vectors.shape
    block_rows, slot_count, block_size, unused_size = hamiltonian.shape
    row_count = lax.axis_size("row")
    first_row = lax.axis_index("row") * block_rows
    local_cols = (column_blocks - first_row + block_rows) % (block_rows * row_count)

    def apply_field(operand):
        widened = with_halo(operand, (("row", 0),), block_rows * block_size)
        widened_blocks = widened.reshape(3 * block_rows, block_size, panel_cols)
        picked = jnp.take(widened_blocks, local_cols, axis=0)
        live_mask = (
            jnp.arange(slot_count, dtype=jnp.int32)[None, :] < live_counts[:, None]
        ).astype(jnp.float32)
        summed = jnp.einsum(
            "rkij,rkjc->ric",
            hamiltonian,
            picked * live_mask[:, :, None, None],
            precision=lax.Precision.HIGHEST,
            preferred_element_type=jnp.float32,
        )
        return summed.reshape(rows_dev, panel_cols)

    centre = (upper_bound[0] + lower_bound[0]) / 2
    radius = (upper_bound[0] - lower_bound[0]) / 2
    first = (apply_field(vectors) - centre * vectors) / radius
    second = 2 * (apply_field(first) - centre * first) / radius - vectors
    energy = lax.psum(jnp.sum(second * second), ("row", "vec"))
    current = second * jnp.sqrt(NV / (4 * (energy + 1e-06)))
    stacked = current
    for iteration in range(NS_ITERS):
        stacked = lax.all_to_all(current, "vec", split_axis=0, concat_axis=1, tiled=True)
        local_gram = jnp.einsum(
            "rc,rd->cd",
            stacked,
            stacked,
            precision=lax.Precision.HIGHEST,
            preferred_element_type=jnp.float32,
        )
        gram = lax.psum(local_gram, ("row", "vec"))
        stacked = 1.5 * stacked - 0.5 * jnp.dot(
            stacked, gram, precision=lax.Precision.HIGHEST, preferred_element_type=jnp.float32
        )
        current = lax.all_to_all(stacked, "vec", split_axis=1, concat_axis=0, tiled=True)
    total_rows = rows_dev * row_count
    return current * math.sqrt(total_rows)


def solution(mesh):
    placed = (P("row", "vec"), P("row", None, None, None), P("row", None), P("row"), P(), P())
    return jax.shard_map(
        on_device, mesh=mesh, in_specs=placed, out_specs=P("row", "vec"), check_vma=False
    )
```

profile of v0, /device:TPU:1, one launch (start us, length us, event | category | flops | bytes accessed | tf_op | source)
XLA Modules:
  0.0 796.7 jit_solution(12494661973624520224)
XLA Ops:
  6.5 6.8 collective-permute-start.1
  14.6 0.8 compare_and_fusion
  15.5 20.0 %collective-permute-done.1 = f32[2048,128]{1,0:T(8,128)S(1)} collective-permute-done((f32[2048,128]{1,0:T(8,128)}, f32[2048,128]{1,0:T(8,128)S(1)}, u32[]{:S(2)}, u32[]{:S(2)}) %collective-permute-start.1) | collective-permute-done | bytes 1048608 | tf_op jit(solution)/shard_map/ppermute | solution.py:20
  35.5 1.0 copy-done.4
  36.4 4.3 collective-permute-done
  40.7 2.1 pad_maximum_fusion
  42.8 5.9 gather_fusion
  48.7 19.3 %fusion.1 = f32[16,128,128,1]{1,2,3,0:T(8,128)S(1)} fusion(f32[16,12,128,128]{3,2,1,0:T(8,128)} %param.9, f32[16,12,128,128]{3,2,1,0:T(8,128)} %bitcast.112, f32[16,12]{1,0:T(8,128)S(1)} %get-tuple-element.10, pred[16,12]{1,0:T(8,128)(4,1)S(1)} %get-tuple-element.8), kind=kOutput, calls=%fused_computation.5 | convolution fusion | flops 4838129664 | bytes 26215360 | tf_op jit(solution)/shard_map/rkij,rkjc->ric/dot_general | solution.py:41
  68.1 1.2 collective-permute-start.3
  69.4 0.3 collective-permute-start.2
  69.7 21.4 %collective-permute-done.3 = f32[2048,128]{1,0:T(8,128)S(1)} collective-permute-done((f32[2048,128]{1,0:T(8,128)S(1)}, f32[2048,128]{1,0:T(8,128)S(1)}, u32[]{:S(2)}, u32[]{:S(2)}) %collective-permute-start.3) | collective-permute-done | bytes 1048608 | tf_op jit(solution)/shard_map/ppermute | solution.py:20
  91.1 4.5 collective-permute-done.2
  95.8 5.9 gather_fusion.1
  101.7 19.4 %fusion = f32[16,128,128,1]{1,2,3,0:T(8,128)S(1)} fusion(f32[16,12,128,128]{3,2,1,0:T(8,128)} %param.9, f32[16,12,128,128]{3,2,1,0:T(8,128)} %bitcast.111, f32[16,12]{1,0:T(8,128)S(1)} %get-tuple-element.10, pred[16,12]{1,0:T(8,128)(4,1)S(1)} %get-tuple-element.8), kind=kOutput, calls=%fused_computation.3 | convolution fusion | flops 4838129664 | bytes 26215360 | tf_op jit(solution)/shard_map/rkij,rkjc->ric/dot_general | solution.py:41
  121.1 1.0 multiply_reduce_fusion
  122.1 65.0 %psum.28 = f32[]{:T(128)} all-reduce(f32[]{:T(128)} %get-tuple-element.6), channel_id=1, replica_groups=mesh['row'=16,'vec'=8] {'row','vec'}, use_global_device_ids=true, to_apply=%region_1.3 | all-reduce | flops 1 | bytes 8 | tf_op jit(solution)/shard_map/psum | solution.py:54
  187.9 19.4 %all_to_all.96 = f32[8,256,128]{2,1,0:T(8,128)S(1)} all-to-all(f32[8,256,128]{2,1,0:T(8,128)S(1)} %bitcast.113), channel_id=1, replica_groups=mesh['row'=16,'vec'=8] {'vec'}, dimensions={0} | all-to-all | bytes 2097152 | tf_op jit(solution)/shard_map/all_to_all | solution.py:58
  207.2 5.1 fusion.21
  212.4 150.4 %all-reduce.4.cloned.1.call-done = f32[1024,1024]{1,0:T(8,128)} async-done(((f32[1024,1024]{1,0:T(8,128)}), f32[1024,1024]{1,0:T(8,128)}) %all-reduce.4.cloned.1.call-update) | async-done | bytes 4194320 | tf_op jit(solution)/shard_map/psum | solution.py:66
  362.8 5.8 fusion.13
  368.7 19.7 %all_to_all.97 = f32[256,8,128]{2,0,1:T(8,128)S(1)} all-to-all(f32[256,8,128]{2,0,1:T(8,128)S(1)} %bitcast.114), channel_id=1, replica_groups=mesh['row'=16,'vec'=8] {'vec'}, dimensions={1} | all-to-all | bytes 2097152 | tf_op jit(solution)/shard_map/all_to_all | solution.py:70
  388.4 18.4 %all_to_all.98 = f32[8,256,128]{2,1,0:T(8,128)S(1)} all-to-all(f32[8,256,128]{2,1,0:T(8,128)S(1)} %bitcast.115), channel_id=1, replica_groups=mesh['row'=16,'vec'=8] {'vec'}, dimensions={0} | all-to-all | bytes 2097152 | tf_op jit(solution)/shard_map/all_to_all | solution.py:58
  406.8 5.1 fusion.18
  411.9 151.2 %all-reduce.6.cloned.1.call-done = f32[1024,1024]{1,0:T(8,128)} async-done(((f32[1024,1024]{1,0:T(8,128)}), f32[1024,1024]{1,0:T(8,128)}) %all-reduce.6.cloned.1.call-update) | async-done | bytes 4194320 | tf_op jit(solution)/shard_map/psum | solution.py:66
  563.1 5.8 fusion.11
  569.0 19.7 %all_to_all.99 = f32[256,8,128]{2,0,1:T(8,128)S(1)} all-to-all(f32[256,8,128]{2,0,1:T(8,128)S(1)} %bitcast.116), channel_id=1, replica_groups=mesh['row'=16,'vec'=8] {'vec'}, dimensions={1} | all-to-all | bytes 2097152 | tf_op jit(solution)/shard_map/all_to_all | solution.py:70
  588.7 18.4 %all_to_all.100 = f32[8,256,128]{2,1,0:T(8,128)S(1)} all-to-all(f32[8,256,128]{2,1,0:T(8,128)S(1)} %bitcast.117), channel_id=1, replica_groups=mesh['row'=16,'vec'=8] {'vec'}, dimensions={0} | all-to-all | bytes 2097152 | tf_op jit(solution)/shard_map/all_to_all | solution.py:58
  607.1 5.1 fusion.15
  612.2 151.4 %all-reduce.8.cloned.1.call-done = f32[1024,1024]{1,0:T(8,128)} async-done(((f32[1024,1024]{1,0:T(8,128)}), f32[1024,1024]{1,0:T(8,128)}) %all-reduce.8.cloned.1.call-update) | async-done | bytes 4194320 | tf_op jit(solution)/shard_map/psum | solution.py:66
  763.5 5.8 fusion.9
  769.4 19.7 %all_to_all.101 = f32[256,8,128]{2,0,1:T(8,128)S(1)} all-to-all(f32[256,8,128]{2,0,1:T(8,128)S(1)} %bitcast.118), channel_id=1, replica_groups=mesh['row'=16,'vec'=8] {'vec'}, dimensions={1} | all-to-all | bytes 2097152 | tf_op jit(solution)/shard_map/all_to_all | solution.py:70
  789.1 1.1 broadcast_multiply_fusion
  (24 shorter events, 0.9 us)
Async XLA Ops:
  6.5 356.3 %all-reduce.4.cloned.1.call-start = ((), (), s32[]{:S(2)}) async-start(), calls=%async_computation.6 | async-start | bytes 8388608 | tf_op jit(solution)/shard_map/psum | solution.py:66
  6.5 28.9 %collective-permute-start.1 = (f32[2048,128]{1,0:T(8,128)}, f32[2048,128]{1,0:T(8,128)S(1)}, u32[]{:S(2)}, u32[]{:S(2)}) collective-permute-start(f32[2048,128]{1,0:T(8,128)} %param.8), channel_id=1, source_target_pairs={{8,0},{16,8},{24,16},{32,24},{40,32},{48,40},{56,48},{64,56},{72,6... | collective-permute-start | bytes 3145736 | tf_op jit(solution)/shard_map/ppermute | solution.py:20
  13.3 27.4 %collective-permute-start = (f32[2048,128]{1,0:T(8,128)}, f32[2048,128]{1,0:T(8,128)}, u32[]{:S(2)}, u32[]{:S(2)}) collective-permute-start(f32[2048,128]{1,0:T(8,128)} %param.8), channel_id=1, source_target_pairs={{0,8},{8,16},{16,24},{24,32},{32,40},{40,48},{48,56},{56,64},{64,7... | collective-permute-start | bytes 3145736 | tf_op jit(solution)/shard_map/ppermute | solution.py:18
  35.5 1.0 copy-start.4
  48.7 19.3 %copy-start.2 = (f32[2048,128]{1,0:T(8,128)S(1)}, f32[2048,128]{1,0:T(8,128)}, u32[]{:S(2)}) copy-start(f32[2048,128]{1,0:T(8,128)} %param.8) | copy-start | bytes 3145732
  68.0 27.8 %copy-start = (f32[16,128,128,1]{1,2,3,0:T(8,128)}, f32[16,128,128,1]{1,2,3,0:T(8,128)S(1)}, u32[]{:S(2)}) copy-start(f32[16,128,128,1]{1,2,3,0:T(8,128)S(1)} %fusion.1) | copy-start | bytes 3145732
  68.1 23.0 %collective-permute-start.3 = (f32[2048,128]{1,0:T(8,128)S(1)}, f32[2048,128]{1,0:T(8,128)S(1)}, u32[]{:S(2)}, u32[]{:S(2)}) collective-permute-start(f32[2048,128]{1,0:T(8,128)S(1)} %fusion.26), channel_id=1, source_target_pairs={{8,0},{16,8},{24,16},{32,24},{40,32},{48,40},{56,48},{64,56},{72,6... | collective-permute-start | bytes 3145736 | tf_op jit(solution)/shard_map/ppermute | solution.py:20
  69.4 26.2 %collective-permute-start.2 = (f32[2048,128]{1,0:T(8,128)S(1)}, f32[2048,128]{1,0:T(8,128)S(1)}, u32[]{:S(2)}, u32[]{:S(2)}) collective-permute-start(f32[2048,128]{1,0:T(8,128)S(1)} %fusion.26), channel_id=1, source_target_pairs={{0,8},{8,16},{16,24},{24,32},{32,40},{40,48},{48,56},{56,64},{64,7... | collective-permute-start | bytes 3145736 | tf_op jit(solution)/shard_map/ppermute | solution.py:18
  101.7 19.4 %copy-start.1 = (f32[16,128,128,1]{1,2,3,0:T(8,128)S(1)}, f32[16,128,128,1]{1,2,3,0:T(8,128)}, u32[]{:S(2)}) copy-start(f32[16,128,128,1]{1,2,3,0:T(8,128)} %copy-done) | copy-start | bytes 3145732
  101.7 19.4 %copy-start.3 = (f32[2048,128]{1,0:T(8,128)S(1)}, f32[2048,128]{1,0:T(8,128)}, u32[]{:S(2)}) copy-start(f32[2048,128]{1,0:T(8,128)} %param.8) | copy-start | bytes 3145732
  212.3 350.8 %all-reduce.6.cloned.1.call-start = ((), (), s32[]{:S(2)}) async-start(), calls=%async_computation.7 | async-start | bytes 8388608 | tf_op jit(solution)/shard_map/psum | solution.py:66
  411.9 351.7 %all-reduce.8.cloned.1.call-start = ((), (), s32[]{:S(2)}) async-start(), calls=%async_computation.8 | async-start | bytes 8388608 | tf_op jit(solution)/shard_map/psum | solution.py:66
Sparse Core Ops, SparseCore 0:
  212.5 150.3 all-reduce.3
  412.0 151.0 all-reduce.5
  612.3 151.1 all-reduce.7
where the time goes:
time: 797 us
  waiting for transfers between devices  503 us (63%)
  blocking collectives  180 us (23%)
  matrix products  71.3 us (9%)
  between operations  15.3 us (2%)
  local copies, waits for them, and re-layouts  13.1 us (2%)
  starting transfers between devices  8.39 us (1%)
    psum x3, waiting for transfers between devices, on_device(): gram = lax.psum(local_gram, ('row', 'vec'))  453 us
    psum x1, blocking collectives, on_device(): energy = lax.psum(jnp.sum(second * second), ('row', 'vec'))  65 us
    all_to_all x3, blocking collectives, on_device(): lax.all_to_all(stacked, 'vec', split_axis=1, concat_axis=0, tiled=True)  59.1 us
    all_to_all x3, blocking collectives, on_device(): lax.all_to_all(current, 'vec', split_axis=0, concat_axis=1, tiled=True)  56.1 us
    ppermute x2, waiting for transfers between devices, with_halo(): lax.ppermute(head, axis, [((i + 1) % count, i) for i in range(count)])  41.4 us
    dot_general x2, matrix products, apply_field(): jnp.einsum('rkij,rkjc->ric', hamiltonian, picked * live_mask[:, :, None,...  38.7 us
    dot_general x3, matrix products, on_device(): jnp.dot(stacked, gram, precision=lax.Precision.HIGHEST, preferred_element...  17.4 us
  transfers between devices with their start and end apart: 7, of which 7 were waited for; matrix products, arithmetic and copies ran while one was open for 0% of the time, Pallas kernels for 0%

commit v1 on v0

--- a/solution.py
+++ b/solution.py
@@ -63,7 +63,7 @@
             precision=lax.Precision.HIGHEST,
             preferred_element_type=jnp.float32,
         )
-        gram = lax.psum(local_gram, ("row", "vec"))
+        gram = lax.psum(lax.psum(local_gram, "vec"), "row")
         stacked = 1.5 * stacked - 0.5 * jnp.dot(
             stacked, gram, precision=lax.Precision.HIGHEST, preferred_element_type=jnp.float32
         )

time: 797 us -> 876 us (1.099)
  waiting for transfers between devices: 503 us -> 580 us
    psum x3 -> x6, waiting for transfers between devices: 453 us -> 530 us  [on_device(): gram = lax.psum(lax.psum(local_gram, 'vec'), 'row')]
  transfers between devices with their start and end apart: 7 -> 10, of which waited for: 7 -> 10; matrix products, arithmetic and copies ran while one was open for 0% -> 0% of each run, Pallas kernels for 0% -> 0%
where the time goes in v1:
time: 876 us; the launch traced here: 875 us
  waiting for transfers between devices  580 us (66%)
  blocking collectives  181 us (21%)
  matrix products  71.3 us (8%)
  between operations  15.7 us (2%)
  local copies, waits for them, and re-layouts  13.1 us (1%)
  starting transfers between devices  8.77 us (1%)
    psum x6, waiting for transfers between devices, on_device(): gram = lax.psum(lax.psum(local_gram, 'vec'), 'row')  530 us
    psum x1, blocking collectives, on_device(): energy = lax.psum(jnp.sum(second * second), ('row', 'vec'))  65 us
    all_to_all x3, blocking collectives, on_device(): lax.all_to_all(stacked, 'vec', split_axis=1, concat_axis=0, tiled=True)  60.3 us
    all_to_all x3, blocking collectives, on_device(): lax.all_to_all(current, 'vec', split_axis=0, concat_axis=1, tiled=True)  56.1 us
    ppermute x2, waiting for transfers between devices, with_halo(): lax.ppermute(head, axis, [((i + 1) % count, i) for i in range(count)])  41.4 us
    dot_general x2, matrix products, apply_field(): jnp.einsum('rkij,rkjc->ric', hamiltonian, picked * live_mask[:, :, None,...  38.7 us
  transfers between devices with their start and end apart: 10, of which 10 were waited for; matrix products, arithmetic and copies ran while one was open for 0% of the time, Pallas kernels for 0%

profile of v1, /device:TPU:1, one launch (start us, length us, event | category | flops | bytes accessed | tf_op | source)
XLA Modules:
  0.0 875.3 jit_solution(16240763519618186728)
XLA Ops:
  6.5 6.8 collective-permute-start.1
  15.5 20.0 %collective-permute-done.1 = f32[2048,128]{1,0:T(8,128)S(1)} collective-permute-done((f32[2048,128]{1,0:T(8,128)}, f32[2048,128]{1,0:T(8,128)S(1)}, u32[]{:S(2)}, u32[]{:S(2)}) %collective-permute-start.1) | collective-permute-done | bytes 1048608 | tf_op jit(solution)/shard_map/ppermute | solution.py:20
  35.5 1.0 copy-done.4
  36.4 4.3 collective-permute-done
  40.7 2.1 pad_maximum_fusion
  42.8 5.9 gather_fusion
  48.7 19.3 %fusion.1 = f32[16,128,128,1]{1,2,3,0:T(8,128)S(1)} fusion(f32[16,12,128,128]{3,2,1,0:T(8,128)} %param.9, f32[16,12,128,128]{3,2,1,0:T(8,128)} %bitcast.112, f32[16,12]{1,0:T(8,128)S(1)} %get-tuple-element.10, pred[16,12]{1,0:T(8,128)(4,1)S(1)} %get-tuple-element.8), kind=kOutput, calls=%fused_computation.5 | convolution fusion | flops 4838129664 | bytes 26215360 | tf_op jit(solution)/shard_map/rkij,rkjc->ric/dot_general | solution.py:41
  68.1 1.2 collective-permute-start.3
  69.7 21.4 %collective-permute-done.3 = f32[2048,128]{1,0:T(8,128)S(1)} collective-permute-done((f32[2048,128]{1,0:T(8,128)S(1)}, f32[2048,128]{1,0:T(8,128)S(1)}, u32[]{:S(2)}, u32[]{:S(2)}) %collective-permute-start.3) | collective-permute-done | bytes 1048608 | tf_op jit(solution)/shard_map/ppermute | solution.py:20
  91.1 4.5 collective-permute-done.2
  95.8 5.9 gather_fusion.1
  101.7 19.4 %fusion = f32[16,128,128,1]{1,2,3,0:T(8,128)S(1)} fusion(f32[16,12,128,128]{3,2,1,0:T(8,128)} %param.9, f32[16,12,128,128]{3,2,1,0:T(8,128)} %bitcast.111, f32[16,12]{1,0:T(8,128)S(1)} %get-tuple-element.10, pred[16,12]{1,0:T(8,128)(4,1)S(1)} %get-tuple-element.8), kind=kOutput, calls=%fused_computation.3 | convolution fusion | flops 4838129664 | bytes 26215360 | tf_op jit(solution)/shard_map/rkij,rkjc->ric/dot_general | solution.py:41
  122.1 65.0 %psum.49 = f32[]{:T(128)} all-reduce(f32[]{:T(128)} %get-tuple-element.6), channel_id=1, replica_groups=mesh['row'=16,'vec'=8] {'row','vec'}, use_global_device_ids=true, to_apply=%region_1.3 | all-reduce | flops 1 | bytes 8 | tf_op jit(solution)/shard_map/psum | solution.py:54
  187.8 19.4 %all_to_all.96 = f32[8,256,128]{2,1,0:T(8,128)S(1)} all-to-all(f32[8,256,128]{2,1,0:T(8,128)S(1)} %bitcast.113), channel_id=1, replica_groups=mesh['row'=16,'vec'=8] {'vec'}, dimensions={0} | all-to-all | bytes 2097152 | tf_op jit(solution)/shard_map/all_to_all | solution.py:58
  207.2 5.1 fusion.21
  212.4 66.8 %all-reduce.7.cloned.1.call-done = f32[1024,1024]{1,0:T(8,128)} async-done(((f32[1024,1024]{1,0:T(8,128)}), f32[1024,1024]{1,0:T(8,128)}) %all-reduce.7.cloned.1.call-update) | async-done | bytes 4194320 | tf_op jit(solution)/shard_map/psum | solution.py:66
  279.2 108.5 %all-reduce.9.cloned.1.call-done = f32[1024,1024]{1,0:T(8,128)} async-done(((f32[1024,1024]{1,0:T(8,128)}), f32[1024,1024]{1,0:T(8,128)}) %all-reduce.9.cloned.1.call-update) | async-done | bytes 4194320 | tf_op jit(solution)/shard_map/psum | solution.py:66
  387.7 5.8 fusion.13
  393.6 20.1 %all_to_all.97 = f32[256,8,128]{2,0,1:T(8,128)S(1)} all-to-all(f32[256,8,128]{2,0,1:T(8,128)S(1)} %bitcast.114), channel_id=1, replica_groups=mesh['row'=16,'vec'=8] {'vec'}, dimensions={1} | all-to-all | bytes 2097152 | tf_op jit(solution)/shard_map/all_to_all | solution.py:70
  413.7 18.4 %all_to_all.98 = f32[8,256,128]{2,1,0:T(8,128)S(1)} all-to-all(f32[8,256,128]{2,1,0:T(8,128)S(1)} %bitcast.115), channel_id=1, replica_groups=mesh['row'=16,'vec'=8] {'vec'}, dimensions={0} | all-to-all | bytes 2097152 | tf_op jit(solution)/shard_map/all_to_all | solution.py:58
  432.1 5.1 fusion.18
  437.3 68.9 %all-reduce.11.cloned.1.call-done = f32[1024,1024]{1,0:T(8,128)} async-done(((f32[1024,1024]{1,0:T(8,128)}), f32[1024,1024]{1,0:T(8,128)}) %all-reduce.11.cloned.1.call-update) | async-done | bytes 4194320 | tf_op jit(solution)/shard_map/psum | solution.py:66
  506.2 108.3 %all-reduce.13.cloned.1.call-done = f32[1024,1024]{1,0:T(8,128)} async-done(((f32[1024,1024]{1,0:T(8,128)}), f32[1024,1024]{1,0:T(8,128)}) %all-reduce.13.cloned.1.call-update) | async-done | bytes 4194320 | tf_op jit(solution)/shard_map/psum | solution.py:66
  614.5 5.8 fusion.11
  620.4 20.1 %all_to_all.99 = f32[256,8,128]{2,0,1:T(8,128)S(1)} all-to-all(f32[256,8,128]{2,0,1:T(8,128)S(1)} %bitcast.116), channel_id=1, replica_groups=mesh['row'=16,'vec'=8] {'vec'}, dimensions={1} | all-to-all | bytes 2097152 | tf_op jit(solution)/shard_map/all_to_all | solution.py:70
  640.5 18.4 %all_to_all.100 = f32[8,256,128]{2,1,0:T(8,128)S(1)} all-to-all(f32[8,256,128]{2,1,0:T(8,128)S(1)} %bitcast.117), channel_id=1, replica_groups=mesh['row'=16,'vec'=8] {'vec'}, dimensions={0} | all-to-all | bytes 2097152 | tf_op jit(solution)/shard_map/all_to_all | solution.py:58
  658.9 5.1 fusion.15
  664.3 68.6 %all-reduce.15.cloned.1.call-done = f32[1024,1024]{1,0:T(8,128)} async-done(((f32[1024,1024]{1,0:T(8,128)}), f32[1024,1024]{1,0:T(8,128)}) %all-reduce.15.cloned.1.call-update) | async-done | bytes 4194320 | tf_op jit(solution)/shard_map/psum | solution.py:66
  733.0 108.4 %all-reduce.17.cloned.1.call-done = f32[1024,1024]{1,0:T(8,128)} async-done(((f32[1024,1024]{1,0:T(8,128)}), f32[1024,1024]{1,0:T(8,128)}) %all-reduce.17.cloned.1.call-update) | async-done | bytes 4194320 | tf_op jit(solution)/shard_map/psum | solution.py:66
  841.4 5.8 fusion.9
  847.3 20.1 %all_to_all.101 = f32[256,8,128]{2,0,1:T(8,128)S(1)} all-to-all(f32[256,8,128]{2,0,1:T(8,128)S(1)} %bitcast.118), channel_id=1, replica_groups=mesh['row'=16,'vec'=8] {'vec'}, dimensions={1} | all-to-all | bytes 2097152 | tf_op jit(solution)/shard_map/all_to_all | solution.py:70
  867.4 1.1 broadcast_multiply_fusion
  (33 shorter events, 3.3 us)
Async XLA Ops:
  6.5 272.6 %all-reduce.7.cloned.1.call-start = ((), (), s32[]{:S(2)}) async-start(), calls=%async_computation.6 | async-start | bytes 8388608 | tf_op jit(solution)/shard_map/psum | solution.py:66
  6.5 28.9 %collective-permute-start.1 = (f32[2048,128]{1,0:T(8,128)}, f32[2048,128]{1,0:T(8,128)S(1)}, u32[]{:S(2)}, u32[]{:S(2)}) collective-permute-start(f32[2048,128]{1,0:T(8,128)} %param.8), channel_id=1, source_target_pairs={{8,0},{16,8},{24,16},{32,24},{40,32},{48,40},{56,48},{64,56},{72,6... | collective-permute-start | bytes 3145736 | tf_op jit(solution)/shard_map/ppermute | solution.py:20
  13.3 27.4 %collective-permute-start = (f32[2048,128]{1,0:T(8,128)}, f32[2048,128]{1,0:T(8,128)}, u32[]{:S(2)}, u32[]{:S(2)}) collective-permute-start(f32[2048,128]{1,0:T(8,128)} %param.8), channel_id=1, source_target_pairs={{0,8},{8,16},{16,24},{24,32},{32,40},{40,48},{48,56},{56,64},{64,7... | collective-permute-start | bytes 3145736 | tf_op jit(solution)/shard_map/ppermute | solution.py:18
  35.5 1.0 copy-start.4
  48.7 19.3 %copy-start.2 = (f32[2048,128]{1,0:T(8,128)S(1)}, f32[2048,128]{1,0:T(8,128)}, u32[]{:S(2)}) copy-start(f32[2048,128]{1,0:T(8,128)} %param.8) | copy-start | bytes 3145732
  68.0 27.8 %copy-start = (f32[16,128,128,1]{1,2,3,0:T(8,128)}, f32[16,128,128,1]{1,2,3,0:T(8,128)S(1)}, u32[]{:S(2)}) copy-start(f32[16,128,128,1]{1,2,3,0:T(8,128)S(1)} %fusion.1) | copy-start | bytes 3145732
  68.1 23.0 %collective-permute-start.3 = (f32[2048,128]{1,0:T(8,128)S(1)}, f32[2048,128]{1,0:T(8,128)S(1)}, u32[]{:S(2)}, u32[]{:S(2)}) collective-permute-start(f32[2048,128]{1,0:T(8,128)S(1)} %fusion.26), channel_id=1, source_target_pairs={{8,0},{16,8},{24,16},{32,24},{40,32},{48,40},{56,48},{64,56},{72,6... | collective-permute-start | bytes 3145736 | tf_op jit(solution)/shard_map/ppermute | solution.py:20
  69.4 26.2 %collective-permute-start.2 = (f32[2048,128]{1,0:T(8,128)S(1)}, f32[2048,128]{1,0:T(8,128)S(1)}, u32[]{:S(2)}, u32[]{:S(2)}) collective-permute-start(f32[2048,128]{1,0:T(8,128)S(1)} %fusion.26), channel_id=1, source_target_pairs={{0,8},{8,16},{16,24},{24,32},{32,40},{40,48},{48,56},{56,64},{64,7... | collective-permute-start | bytes 3145736 | tf_op jit(solution)/shard_map/ppermute | solution.py:18
  101.7 19.4 %copy-start.1 = (f32[16,128,128,1]{1,2,3,0:T(8,128)S(1)}, f32[16,128,128,1]{1,2,3,0:T(8,128)}, u32[]{:S(2)}) copy-start(f32[16,128,128,1]{1,2,3,0:T(8,128)} %copy-done) | copy-start | bytes 3145732
  101.7 19.4 %copy-start.3 = (f32[2048,128]{1,0:T(8,128)S(1)}, f32[2048,128]{1,0:T(8,128)}, u32[]{:S(2)}) copy-start(f32[2048,128]{1,0:T(8,128)} %param.8) | copy-start | bytes 3145732
  212.3 175.4 %all-reduce.9.cloned.1.call-start = ((), (), s32[]{:S(2)}) async-start(), calls=%async_computation.7 | async-start | bytes 8388608 | tf_op jit(solution)/shard_map/psum | solution.py:66
  279.2 226.9 %all-reduce.11.cloned.1.call-start = ((), (), s32[]{:S(2)}) async-start(), calls=%async_computation.8 | async-start | bytes 8388608 | tf_op jit(solution)/shard_map/psum | solution.py:66
  437.2 177.3 %all-reduce.13.cloned.1.call-start = ((), (), s32[]{:S(2)}) async-start(), calls=%async_computation.9 | async-start | bytes 8388608 | tf_op jit(solution)/shard_map/psum | solution.py:66
  506.2 226.8 %all-reduce.15.cloned.1.call-start = ((), (), s32[]{:S(2)}) async-start(), calls=%async_computation.10 | async-start | bytes 8388608 | tf_op jit(solution)/shard_map/psum | solution.py:66
  664.0 177.3 %all-reduce.17.cloned.1.call-start = ((), (), s32[]{:S(2)}) async-start(), calls=%async_computation.11 | async-start | bytes 8388608 | tf_op jit(solution)/shard_map/psum | solution.py:66
Sparse Core Ops, SparseCore 0:
  212.4 66.6 all-reduce.6
  282.5 105.1 all-reduce.8
  437.3 68.7 all-reduce.10
  509.3 105.1 all-reduce.12
  664.1 68.7 all-reduce.14
  736.2 105.1 all-reduce.16
